TPU v7x, 32 devices: a whole 2x2x4 slice. The times are simulated.
32 devices in a mesh: chain: 4 (over x, core), band: 8 (over z, y).
Axes of the slice: x: 2, y: 2, z: 4, core: 2. Of those that a mesh axis runs over, the one named last changes fastest.
Arguments:
- diag_inverse: float32 [8192, 2048], P(('chain', 'band'))
- coupling: float32 [8192, 2048], P('chain', 'band'), may hold values from -0.09375 to 0.09375
- elem_stiff: float32 [24, 24, 16384], P(None, None, ('chain', 'band')), may hold values from -6 to 6
- elem_mass: float32 [24, 24, 16384], P(None, None, ('chain', 'band')), may hold values from -6 to 6
- elem_dofs: int32 [24, 16384], P(None, ('chain', 'band')), may hold values from 0 to 2047
- elem_slab: int32 [16384, 1], P(('chain', 'band')), may hold values from 0 to 3; in each aligned block of 512 rows (0 to 511, 512 to 1023, ...) at most 256 rows name the same one
- elem_var: int32 [16384], P(('chain', 'band')), may hold values from 0 to 191
- mode: float32 [8192], P(('chain', 'band')), may hold values from -0.4 to 0.4
- mass_mode: float32 [8192], P('chain'), may hold values from -1.2 to 1.2
- eigenvalue: float32 [1], replicated, may hold values from 0.5 to 2
Outputs:
- eigvec_slope: float32 [192, 8192], P(None, ('chain', 'band'))
- eigval_slope: float32 [192], replicated
Inputs may be any that keep to these rules, and one draw needn't show every extreme that they name: `elem_slab`: within the rows of one device no slab is named by more than 256 elements, a bound that some block reaches.
All inputs are finite; a program needn't handle non-finite values.
Results may differ from a plain program's by a relative error of at most 0.00014.
Values sent between devices are 32-bit elements; how exact they have to be, the bound alone decides.
No kernel may reach another device: no remote copies, remote signals or barrier semaphores. Data moves between devices by JAX's collectives and lax.ppermute only.
A program may use at most 64 MiB of HBM per device.

v0:
```python
import jax
import jax.numpy as jnp
from jax import lax
from jax.sharding import PartitionSpec as P

VARS = 192
PANELS = 4


def from_behind(value, axis, by):
    size = lax.axis_size(axis)
    pairs = [(i, i + by) for i in range(size) if 0 <= i + by < size]
    return lax.ppermute(value, axis, pairs)


def sweep(stored, shift_by, iterations, panel_rows, piece_cols, prepare, finish):

    def advance(iteration, carry):
        outgoing, kept = carry
        received = from_behind(outgoing, "chain", shift_by)
        partial_value, context = prepare(iteration, received, kept)
        summed = lax.psum(partial_value, "band")
        return finish(iteration, summed, context, kept)

    outgoing = jnp.zeros((panel_rows, piece_cols), jnp.float32)
    return lax.fori_loop(0, iterations, advance, (outgoing, stored))[1]


def on_device(
    diag_inverse,
    coupling,
    elem_stiff,
    elem_mass,
    elem_dofs,
    elem_slab,
    elem_var,
    mode,
    mass_mode,
    eigenvalue,
):
    highest = lax.Precision.HIGHEST
    chain_len = lax.axis_size("chain")
    chain_pos = lax.axis_index("chain")
    band_pos = lax.axis_index("band")
    piece_cols = diag_inverse.shape[0]
    slab_rows = diag_inverse.shape[1]
    elem_width = elem_dofs.shape[0]
    elem_count = elem_dofs.shape[1]
    capacity = 2 * elem_count // chain_len
    eigen_val = eigenvalue[0]
    whole_mode = lax.all_gather(mode, ("chain", "band"), axis=0, tiled=True)
    dest_slab = elem_slab[:, 0]
    dof_index = dest_slab[None, :] * slab_rows + elem_dofs
    mode_at = whole_mode[dof_index]
    operator = elem_stiff - eigen_val * elem_mass
    loads = -jnp.einsum("ije,je->ie", operator, mode_at, precision=highest)
    quadratic = -jnp.sum(mode_at * loads, axis=0)
    matches = (elem_var[None, :] == jnp.arange(VARS)[:, None]).astype(jnp.float32)
    local_slope = jnp.dot(matches, quadratic, precision=highest)
    eigval_slope = lax.psum(local_slope, ("chain", "band"))
    onehot = (dest_slab[:, None] == jnp.arange(chain_len)[None, :]).astype(jnp.int32)
    slot_rank = jnp.sum((jnp.cumsum(onehot, axis=0) - 1) * onehot, axis=1)
    flat_index = elem_var[None, :] * slab_rows + elem_dofs
    send_values = (
        jnp.zeros((chain_len, elem_width, capacity), jnp.float32)
        .at[dest_slab, :, slot_rank]
        .set(loads.T)
    )
    send_index = (
        jnp.zeros((chain_len, elem_width, capacity), jnp.int32)
        .at[dest_slab, :, slot_rank]
        .set(flat_index.T)
    )
    got_values, got_index = (
        lax.all_to_all(send_values, "chain", split_axis=0, concat_axis=0, tiled=True),
        lax.all_to_all(send_index, "chain", split_axis=0, concat_axis=0, tiled=True),
    )
    assembled = (
        jnp.zeros((VARS * slab_rows,), jnp.float32)
        .at[got_index.reshape(-1)]
        .add(got_values.reshape(-1))
    )
    assembled = assembled.reshape(VARS, slab_rows)
    slope_term = eigval_slope[:, None] * mass_mode[None, :]
    panel_count = PANELS
    panel_rows = VARS // panel_count
    iterations = chain_len + panel_count - 1
    contract = (((1,), (1,)), ((), ()))

    def locate(panel_index):
        active = (panel_index >= 0) & (panel_index < panel_count)
        first_row = jnp.clip(panel_index, 0, panel_count - 1) * panel_rows
        return (active, first_row)

    def place(kept, fresh, active, first_row):
        previous = lax.dynamic_slice_in_dim(kept, first_row, panel_rows, 0)
        return lax.dynamic_update_slice_in_dim(
            kept, jnp.where(active, fresh, previous), first_row, 0
        )

    def forward_prepare(iteration, received, kept):
        active, first_row = locate(iteration - chain_pos)
        rhs_panel = lax.dynamic_slice_in_dim(assembled, first_row, panel_rows, 0)
        carried = lax.dot_general(
            received, coupling, contract, precision=highest, preferred_element_type=jnp.float32
        )
        return (rhs_panel - carried, (active, first_row))

    def forward_finish(iteration, summed, context, kept):
        active, first_row = context
        coupled = summed + lax.dynamic_slice_in_dim(slope_term, first_row, panel_rows, 0)
        fresh = lax.dot_general(
            coupled, diag_inverse, contract, precision=highest, preferred_element_type=jnp.float32
        )
        return (fresh, place(kept, fresh, active, first_row))

    forward_kept = sweep(
        jnp.zeros((VARS, piece_cols), jnp.float32),
        1,
        iterations,
        panel_rows,
        piece_cols,
        forward_prepare,
        forward_finish,
    )

    def backward_prepare(iteration, received, kept):
        active, first_row = locate(iteration - (chain_len - 1 - chain_pos))
        remain = lax.dynamic_slice_in_dim(forward_kept, first_row, panel_rows, 0) - received
        partial_value = jnp.dot(
            remain, diag_inverse, precision=highest, preferred_element_type=jnp.float32
        )
        return (partial_value, (active, first_row))

    def backward_finish(iteration, summed, context, kept):
        active, first_row = context
        own_piece = lax.dynamic_slice_in_dim(summed, band_pos * piece_cols, piece_cols, 1)
        outgoing = jnp.dot(summed, coupling, precision=highest, preferred_element_type=jnp.float32)
        return (outgoing, place(kept, own_piece, active, first_row))

    eigvec_slope = sweep(
        jnp.zeros((VARS, piece_cols), jnp.float32),
        -1,
        iterations,
        panel_rows,
        piece_cols,
        backward_prepare,
        backward_finish,
    )
    return (eigvec_slope, eigval_slope)


def solution(mesh):
    in_specs = (
        P(("chain", "band"), None),
        P("chain", "band"),
        P(None, None, ("chain", "band")),
        P(None, None, ("chain", "band")),
        P(None, ("chain", "band")),
        P(("chain", "band"), None),
        P(("chain", "band")),
        P(("chain", "band")),
        P("chain"),
        P(),
    )
    out_specs = (P(None, ("chain", "band")), P())
    return jax.shard_map(
        on_device, mesh=mesh, in_specs=in_specs, out_specs=out_specs, check_vma=False
    )
```

profile of v0, /device:TPU:0, one launch (start us, length us, event | category | flops | bytes accessed | tf_op | source)
XLA Modules:
  0.0 1581.7 jit_solution(5994299352049603090)
XLA Ops:
  8.7 70.1 %all-gather = f32[32,1,256]{2,1,0:T(1,128)S(1)} all-gather(f32[1,1,256]{2,1,0:T(1,128)} %bitcast.73), channel_id=1, replica_groups=mesh['chain'=4,'band'=8] {'chain','band'}, dimensions={0}, use_global_device_ids=true | all-gather | bytes 33792 | tf_op jit(solution)/shard_map/all_gather | solution.py:51
  78.8 68.0 %gather_fusion = f32[12288]{0:T(1024)S(1)} fusion(f32[8192]{0:T(1024)S(1)} %bitcast.59, s32[12288]{0:T(1024)S(1)} %broadcast_clamp_fusion), kind=kCustom, calls=%fused_computation | custom fusion | bytes 147456 | tf_op jit(solution)/shard_map/gather | solution.py:54
  149.9 24.8 %scatter_fusion.1 = f32[4,24,256]{1,2,0:T(8,128)S(1)} fusion(f32[4,24,256]{1,2,0:T(8,128)S(1)} %broadcast_in_dim.10, s32[512]{0:T(512)S(1)} %bitcast.60, f32[512,24]{1,0:T(8,128)S(1)} %copy.19), kind=kCustom, calls=%fused_computation.2 | custom fusion | bytes 151552 | tf_op jit(solution)/shard_map/scatter | solution.py:67
  179.5 24.8 %scatter_fusion = s32[4,24,256]{1,2,0:T(8,128)S(1)} fusion(s32[4,24,256]{1,2,0:T(8,128)S(1)} %broadcast_in_dim.9, s32[512]{0:T(512)S(1)} %bitcast.61, s32[512,24]{1,0:T(8,128)S(1)} %copy.17), kind=kCustom, calls=%fused_computation.1 | custom fusion | bytes 151552 | tf_op jit(solution)/shard_map/scatter | solution.py:72
  205.1 36.9 %psum.31 = f32[192]{0:T(256)S(1)} all-reduce(f32[192]{0:T(256)S(1)} %bitcast.74), channel_id=1, replica_groups=mesh['chain'=4,'band'=8] {'chain','band'}, use_global_device_ids=true, to_apply=%region_7.8 | all-reduce | flops 192 | bytes 1536 | tf_op jit(solution)/shard_map/psum | solution.py:60
  250.0 159.9 %scatter_custom_fusion.2 = f32[393216]{0:T(1024)} fusion(s32[24576]{0:T(1024)S(1)} %bitcast.66, f32[24576]{0:T(1024)S(1)} %bitcast.65, f32[]{:T(128)} %constant.139.clone.1), kind=kCustom, calls=%fused_computation.17 | custom fusion | flops 24576 | bytes 1572868 | tf_op jit(solution)/shard_map/scatter-add | solution.py:81
  412.7 590.1 %while.32 = (s32[]{:T(128)}, f32[48,256]{1,0:T(8,128)S(1)}, f32[192,256]{1,0:T(8,128)S(1)}, s32[]{:T(128)}, f32[192,2048]{1,0:T(8,128)}, /*index=5*/f32[2048,256...) while((s32[]{:T(128)}, f32[48,256]{1,0:T(8,128)S(1)}, ...), condition=%wide.region_10.11_spmd, body=%wide.region_8.10_spmd.sunk | while | flops 604286976 | bytes 8521536 | solution.py:26
  419.0 75.4 %all-reduce.3.cloned.1.call-done = f32[48,2048]{1,0:T(8,128)} async-done(((f32[48,2048]{1,0:T(8,128)}), f32[48,2048]{1,0:T(8,128)}) %all-reduce.3.cloned.1.call-update) | async-done | bytes 393232 | tf_op jit(solution)/shard_map/while/body/eval_jaxpr/psum | solution.py:22
  494.3 3.8 select_dynamic-update-slice_fusion.4
  504.2 74.2 %all-reduce.3.cloned.1.call-done = f32[48,2048]{1,0:T(8,128)} async-done(((f32[48,2048]{1,0:T(8,128)}), f32[48,2048]{1,0:T(8,128)}) %all-reduce.3.cloned.1.call-update) | async-done | bytes 393232 | tf_op jit(solution)/shard_map/while/body/eval_jaxpr/psum | solution.py:22
  588.3 74.2 %all-reduce.3.cloned.1.call-done = f32[48,2048]{1,0:T(8,128)} async-done(((f32[48,2048]{1,0:T(8,128)}), f32[48,2048]{1,0:T(8,128)}) %all-reduce.3.cloned.1.call-update) | async-done | bytes 393232 | tf_op jit(solution)/shard_map/while/body/eval_jaxpr/psum | solution.py:22
  672.5 74.2 %all-reduce.3.cloned.1.call-done = f32[48,2048]{1,0:T(8,128)} async-done(((f32[48,2048]{1,0:T(8,128)}), f32[48,2048]{1,0:T(8,128)}) %all-reduce.3.cloned.1.call-update) | async-done | bytes 393232 | tf_op jit(solution)/shard_map/while/body/eval_jaxpr/psum | solution.py:22
  746.7 3.8 select_dynamic-update-slice_fusion.4
  756.6 74.2 %all-reduce.3.cloned.1.call-done = f32[48,2048]{1,0:T(8,128)} async-done(((f32[48,2048]{1,0:T(8,128)}), f32[48,2048]{1,0:T(8,128)}) %all-reduce.3.cloned.1.call-update) | async-done | bytes 393232 | tf_op jit(solution)/shard_map/while/body/eval_jaxpr/psum | solution.py:22
  840.6 74.2 %all-reduce.3.cloned.1.call-done = f32[48,2048]{1,0:T(8,128)} async-done(((f32[48,2048]{1,0:T(8,128)}), f32[48,2048]{1,0:T(8,128)}) %all-reduce.3.cloned.1.call-update) | async-done | bytes 393232 | tf_op jit(solution)/shard_map/while/body/eval_jaxpr/psum | solution.py:22
  924.7 74.2 %all-reduce.3.cloned.1.call-done = f32[48,2048]{1,0:T(8,128)} async-done(((f32[48,2048]{1,0:T(8,128)}), f32[48,2048]{1,0:T(8,128)}) %all-reduce.3.cloned.1.call-update) | async-done | bytes 393232 | tf_op jit(solution)/shard_map/while/body/eval_jaxpr/psum | solution.py:22
  1002.8 571.6 %while.33 = (s32[]{:T(128)}, f32[48,256]{1,0:T(8,128)S(1)}, f32[192,256]{1,0:T(8,128)S(1)}, s32[]{:T(128)}, f32[192,256]{1,0:T(8,128)S(1)}, /*index=5*/f32[256,2...) while((s32[]{:T(128)}, f32[48,256]{1,0:T(8,128)S(1)}, ...), condition=%wide.region_13.14_spmd, body=%wide.region_11.13_spmd.sunk | while | flops 604102656 | bytes 7831881 | solution.py:26
  1009.8 71.8 %all-reduce.5.cloned.1.call-done = f32[48,2048]{1,0:T(8,128)} async-done(((f32[48,2048]{1,0:T(8,128)}), f32[48,2048]{1,0:T(8,128)}) %all-reduce.5.cloned.1.call-update) | async-done | bytes 393232 | tf_op jit(solution)/shard_map/while/body/eval_jaxpr/psum | solution.py:22
  1091.4 71.9 %all-reduce.5.cloned.1.call-done = f32[48,2048]{1,0:T(8,128)} async-done(((f32[48,2048]{1,0:T(8,128)}), f32[48,2048]{1,0:T(8,128)}) %all-reduce.5.cloned.1.call-update) | async-done | bytes 393232 | tf_op jit(solution)/shard_map/while/body/eval_jaxpr/psum | solution.py:22
  1173.1 71.8 %all-reduce.5.cloned.1.call-done = f32[48,2048]{1,0:T(8,128)} async-done(((f32[48,2048]{1,0:T(8,128)}), f32[48,2048]{1,0:T(8,128)}) %all-reduce.5.cloned.1.call-update) | async-done | bytes 393232 | tf_op jit(solution)/shard_map/while/body/eval_jaxpr/psum | solution.py:22
  1254.7 71.8 %all-reduce.5.cloned.1.call-done = f32[48,2048]{1,0:T(8,128)} async-done(((f32[48,2048]{1,0:T(8,128)}), f32[48,2048]{1,0:T(8,128)}) %all-reduce.5.cloned.1.call-update) | async-done | bytes 393232 | tf_op jit(solution)/shard_map/while/body/eval_jaxpr/psum | solution.py:22
  1336.4 71.8 %all-reduce.5.cloned.1.call-done = f32[48,2048]{1,0:T(8,128)} async-done(((f32[48,2048]{1,0:T(8,128)}), f32[48,2048]{1,0:T(8,128)}) %all-reduce.5.cloned.1.call-update) | async-done | bytes 393232 | tf_op jit(solution)/shard_map/while/body/eval_jaxpr/psum | solution.py:22
  1418.0 71.8 %all-reduce.5.cloned.1.call-done = f32[48,2048]{1,0:T(8,128)} async-done(((f32[48,2048]{1,0:T(8,128)}), f32[48,2048]{1,0:T(8,128)}) %all-reduce.5.cloned.1.call-update) | async-done | bytes 393232 | tf_op jit(solution)/shard_map/while/body/eval_jaxpr/psum | solution.py:22
  1499.7 71.8 %all-reduce.5.cloned.1.call-done = f32[48,2048]{1,0:T(8,128)} async-done(((f32[48,2048]{1,0:T(8,128)}), f32[48,2048]{1,0:T(8,128)}) %all-reduce.5.cloned.1.call-update) | async-done | bytes 393232 | tf_op jit(solution)/shard_map/while/body/eval_jaxpr/psum | solution.py:22
  (141 shorter events, 150.6 us)
Async XLA Ops:
  175.5 66.4 %all-to-all-start.1 = ((f32[4,24,256]{2,1,0:T(8,128)}), f32[4,24,256]{2,1,0:T(8,128)S(1)}, u32[]{:S(2)}, u32[]{:S(2)}) async-start(f32[4,24,256]{2,1,0:T(8,128)} %copy.20), calls=%async_computation.1 | async-start | bytes 196608 | tf_op jit(solution)/shard_map/all_to_all | solution.py:75
  241.9 7.8 all-to-all-start
  412.7 81.7 %all-reduce.3.cloned.1.call-start = ((), (), s32[]{:S(2)}) async-start(), calls=%async_computation.2 | async-start | bytes 786432 | tf_op jit(solution)/shard_map/while/body/eval_jaxpr/psum | solution.py:22
  412.7 2.4 collective-permute-start
  498.2 80.2 %all-reduce.3.cloned.1.call-start = ((), (), s32[]{:S(2)}) async-start(), calls=%async_computation.2 | async-start | bytes 786432 | tf_op jit(solution)/shard_map/while/body/eval_jaxpr/psum | solution.py:22
  582.3 80.3 %all-reduce.3.cloned.1.call-start = ((), (), s32[]{:S(2)}) async-start(), calls=%async_computation.2 | async-start | bytes 786432 | tf_op jit(solution)/shard_map/while/body/eval_jaxpr/psum | solution.py:22
  666.4 80.2 %all-reduce.3.cloned.1.call-start = ((), (), s32[]{:S(2)}) async-start(), calls=%async_computation.2 | async-start | bytes 786432 | tf_op jit(solution)/shard_map/while/body/eval_jaxpr/psum | solution.py:22
  750.5 80.2 %all-reduce.3.cloned.1.call-start = ((), (), s32[]{:S(2)}) async-start(), calls=%async_computation.2 | async-start | bytes 786432 | tf_op jit(solution)/shard_map/while/body/eval_jaxpr/psum | solution.py:22
  834.6 80.2 %all-reduce.3.cloned.1.call-start = ((), (), s32[]{:S(2)}) async-start(), calls=%async_computation.2 | async-start | bytes 786432 | tf_op jit(solution)/shard_map/while/body/eval_jaxpr/psum | solution.py:22
  918.7 80.2 %all-reduce.3.cloned.1.call-start = ((), (), s32[]{:S(2)}) async-start(), calls=%async_computation.2 | async-start | bytes 786432 | tf_op jit(solution)/shard_map/while/body/eval_jaxpr/psum | solution.py:22
  1002.9 78.7 %all-reduce.5.cloned.1.call-start = ((), (), s32[]{:S(2)}) async-start(), calls=%async_computation.3 | async-start | bytes 786432 | tf_op jit(solution)/shard_map/while/body/eval_jaxpr/psum | solution.py:22
  1002.9 3.1 collective-permute-start.1
  1084.5 78.7 %all-reduce.5.cloned.1.call-start = ((), (), s32[]{:S(2)}) async-start(), calls=%async_computation.3 | async-start | bytes 786432 | tf_op jit(solution)/shard_map/while/body/eval_jaxpr/psum | solution.py:22
  1084.6 3.1 collective-permute-start.1
  1166.2 78.7 %all-reduce.5.cloned.1.call-start = ((), (), s32[]{:S(2)}) async-start(), calls=%async_computation.3 | async-start | bytes 786432 | tf_op jit(solution)/shard_map/while/body/eval_jaxpr/psum | solution.py:22
  1166.2 3.1 collective-permute-start.1
  1247.8 78.7 %all-reduce.5.cloned.1.call-start = ((), (), s32[]{:S(2)}) async-start(), calls=%async_computation.3 | async-start | bytes 786432 | tf_op jit(solution)/shard_map/while/body/eval_jaxpr/psum | solution.py:22
  1247.9 3.1 collective-permute-start.1
  1329.5 78.7 %all-reduce.5.cloned.1.call-start = ((), (), s32[]{:S(2)}) async-start(), calls=%async_computation.3 | async-start | bytes 786432 | tf_op jit(solution)/shard_map/while/body/eval_jaxpr/psum | solution.py:22
  1329.5 3.1 collective-permute-start.1
  1411.1 78.7 %all-reduce.5.cloned.1.call-start = ((), (), s32[]{:S(2)}) async-start(), calls=%async_computation.3 | async-start | bytes 786432 | tf_op jit(solution)/shard_map/while/body/eval_jaxpr/psum | solution.py:22
  1411.2 3.1 collective-permute-start.1
  1492.8 78.7 %all-reduce.5.cloned.1.call-start = ((), (), s32[]{:S(2)}) async-start(), calls=%async_computation.3 | async-start | bytes 786432 | tf_op jit(solution)/shard_map/while/body/eval_jaxpr/psum | solution.py:22
  1492.8 3.1 collective-permute-start.1
  (14 other events, 422.1 us)
Sparse Core Ops, SparseCore 0:
  419.1 75.2 all-reduce.2
  504.3 74.0 all-reduce.2
  588.4 74.0 all-reduce.2
  672.6 74.0 all-reduce.2
  756.7 74.0 all-reduce.2
  840.8 74.0 all-reduce.2
  924.9 74.0 all-reduce.2
  1009.9 71.6 all-reduce.4
  1091.5 71.6 all-reduce.4
  1173.2 71.6 all-reduce.4
  1254.8 71.6 all-reduce.4
  1336.5 71.6 all-reduce.4
  1418.1 71.6 all-reduce.4
  1499.8 71.6 all-reduce.4
where the time goes:
time: 1580 us
  waiting for transfers between devices  1050 us (66%)
  other arithmetic  171 us (11%)
  local copies, waits for them, and re-layouts  123 us (8%)
  blocking collectives  107 us (7%)
  matrix products  94.3 us (6%)
  starting transfers between devices  25.9 us (2%)
    psum x14, waiting for transfers between devices, advance(): summed = lax.psum(partial_value, 'band')  1020 us
    scatter-add x1, other arithmetic, on_device(): assembled = jnp.zeros((VARS * slab_rows,), jnp.float32).at[got_index.resh...  160 us
    all_gather x1, blocking collectives, on_device(): whole_mode = lax.all_gather(mode, ('chain', 'band'), axis=0, tiled=True)  70.1 us
    gather x2, local copies, waits for them, and re-layouts, on_device(): mode_at = whole_mode[dof_index]  68 us
    psum x1, blocking collectives, on_device(): eigval_slope = lax.psum(local_slope, ('chain', 'band'))  36.9 us
  transfers between devices with their start and end apart: 30, of which 29 were waited for; matrix products, arithmetic and copies ran while one was open for 2% of the time, Pallas kernels for 0%

commit v1 on v0

v1 whole, which is shorter than its diff:
```python
import functools

import jax
import jax.numpy as jnp
from jax import lax
from jax.experimental import pallas as pl
from jax.experimental.pallas import tpu as pltpu
from jax.sharding import PartitionSpec as P

VARS = 192
LANES = 128
CHUNK = 256
HBM = pl.BlockSpec(memory_space=pl.ANY)
VMEM = pl.BlockSpec(memory_space=pltpu.VMEM)
SMEM = pl.BlockSpec(memory_space=pltpu.SMEM)
NN = (((1,), (0,)), ((), ()))
NT = (((1,), (1,)), ((), ()))
BF16, F32, I32 = jnp.bfloat16, jnp.float32, jnp.int32


def round_up(n, m):
    return -(-n // m) * m


def halves(x):
    hi = x.astype(BF16)
    return hi, (x - hi.astype(F32)).astype(BF16)


def mul(a, b, dims):
    return lax.dot_general(a, b, dims, preferred_element_type=F32)


def mul3(a, b, dims):
    (ah, al), (bh, bl) = a, b
    return mul(ah, bh, dims) + (mul(al, bh, dims) + mul(ah, bl, dims))


def loads_kernel(groups, lam_ref, mode_ref, dofs_ref, slab_ref, var_ref, stiff_ref, mass_ref, out_ref, x_ref):
    width, count = dofs_ref.shape
    rows = mode_ref.shape[0]
    per_slab = rows // groups
    per_group = VARS // groups
    lam = lam_ref[0]
    dofs = dofs_ref[...]
    high = slab_ref[...] * per_slab + (dofs >> 7)
    low = dofs & (LANES - 1)
    spans = [slice(s, s + LANES) for s in range(0, count, LANES)]

    def look(r, found):
        row = jnp.broadcast_to(mode_ref[pl.ds(r, 1), :], (width, LANES))
        return tuple(
            jnp.where(high[:, s] == r, jnp.take_along_axis(row, low[:, s], axis=1), f)
            for s, f in zip(spans, found)
        )

    zero = jnp.zeros((width, LANES), F32)
    mode_at = jnp.concatenate(lax.fori_loop(0, rows, look, tuple(zero for _ in spans)), axis=1)
    quad = jnp.zeros((1, count), F32)
    x_ref[...] = jnp.zeros_like(x_ref)
    for i in range(width):
        load = -jnp.sum((stiff_ref[i] - lam * mass_ref[i]) * mode_at, axis=0, keepdims=True)
        quad = quad - mode_at[i : i + 1] * load
        x_ref[i : i + 1, :] = load
    var = var_ref[...]
    x_ref[width : 2 * width, :] = dofs.astype(F32)
    x_ref[2 * width : 2 * width + 1, :] = quad
    x_ref[2 * width + 1 : 2 * width + 2, :] = var.astype(F32)
    x_ref[2 * width + 2 : 2 * width + 3, :] = slab_ref[...].astype(F32)

    group = jnp.zeros_like(var)
    for g in range(1, groups):
        group = group + (var >= g * per_group).astype(I32)
    ids = lax.broadcasted_iota(I32, (8, count), 0)
    member = (ids == group).astype(F32)
    before = lax.broadcasted_iota(I32, (count, count), 0)
    after = lax.broadcasted_iota(I32, (count, count), 1)
    rank = mul(member.astype(BF16), (before < after).astype(F32).astype(BF16), NN)
    total = jnp.sum(member, axis=1, keepdims=True)
    offset = jnp.where(ids < group, total, 0.0)
    slot = jnp.sum(member * rank + offset, axis=0, keepdims=True).astype(I32)
    place = (before == slot).astype(F32).astype(BF16)
    x = x_ref[...]
    hi = x.astype(BF16)
    rest = x - hi.astype(F32)
    mid = rest.astype(BF16)
    low_part = (rest - mid.astype(F32)).astype(BF16)
    moved = mul(hi, place, NT) + (mul(mid, place, NT) + mul(low_part, place, NT))
    out_ref[...] = moved[: out_ref.shape[0]]


def element_loads(groups, lam, mode, dofs, slab, var, stiff, mass):
    width, count = dofs.shape
    features = round_up(2 * width + 3, 8)
    return pl.pallas_call(
        functools.partial(loads_kernel, groups),
        out_shape=jax.ShapeDtypeStruct((features, count), F32),
        in_specs=[SMEM] + [VMEM] * 6,
        out_specs=VMEM,
        scratch_shapes=[pltpu.VMEM((round_up(features, 16), count), F32)],
        name="loads",
    )(lam, mode, dofs, slab, var, stiff, mass)


def assemble_kernel(width, band, me_ref, feat_ref, mass_ref, first_ref, rest_ref, cols_ref, e_ref, v_ref, r_ref):
    sources, features, count = feat_ref.shape
    slabs, slab_cols = mass_ref.shape
    group_rows = VARS // sources
    piece = slab_cols // band
    me = me_ref[0]
    base = (me * group_rows).astype(F32)
    codes = v_ref.shape[1]
    nth = lax.broadcasted_iota(I32, (8, slab_cols), 1)
    code_at = lax.broadcasted_iota(I32, (8, codes), 1)
    e_ref_lanes = slab_cols + LANES

    def tile(s, t, filled):
        src = pl.ds(pl.multiple_of(t * 8, 8), 8)
        dst = pl.ds(pl.multiple_of(filled * 8, 8), 8)
        item = cols_ref[s, src, :]
        total = jnp.zeros((8, slab_cols), F32)
        for i in range(width):
            dof = item[:, width + i : width + i + 1].astype(I32)
            total = total + jnp.where(nth == dof, item[:, i : i + 1], 0.0)
        e_ref[dst, :slab_cols] = total
        e_ref[dst, slab_cols:] = jnp.broadcast_to(item[:, 2 * width : 2 * width + 1], (8, LANES))
        var = item[:, 2 * width + 1 : 2 * width + 2] - base
        slab = item[:, 2 * width + 2 : 2 * width + 3]
        held = (var >= 0.0) & (var < group_rows)
        code = jnp.where(held, slab * group_rows + var, -1.0).astype(I32)
        v_ref[dst, :] = (code_at == code).astype(F32)
        return filled + 1

    filled = jnp.int32(0)
    for s in range(sources):
        pad = cols_ref.shape[2] - features
        block = jnp.concatenate([feat_ref[s], jnp.zeros((pad, count), F32)], axis=0)
        cols_ref[s] = block.T
        var_row = feat_ref[s, 2 * width + 1 : 2 * width + 2, :]
        start = jnp.sum((var_row < base).astype(F32)).astype(I32)
        stop = jnp.sum((var_row < base + group_rows).astype(F32)).astype(I32)
        filled = lax.fori_loop(start >> 3, (stop + 7) >> 3, functools.partial(tile, s), filled)
    chunks = (filled * 8 + CHUNK - 1) // CHUNK

    def blank(t, _):
        dst = pl.ds(pl.multiple_of(t * 8, 8), 8)
        e_ref[dst, :] = jnp.zeros((8, e_ref_lanes), F32)
        v_ref[dst, :] = jnp.zeros((8, codes), F32)
        return 0

    lax.fori_loop(filled, chunks * (CHUNK // 8), blank, 0)
    r_ref[...] = jnp.zeros_like(r_ref)

    def gather(j, _):
        rows = pl.ds(pl.multiple_of(j * CHUNK, CHUNK), CHUNK)
        picks = v_ref[rows, :].T.astype(BF16)
        for lo in range(0, e_ref_lanes, 512):
            hi_ = min(lo + 512, e_ref_lanes)
            eh, el = halves(e_ref[rows, lo:hi_])
            r_ref[:, lo:hi_] += mul(picks, eh, NN) + mul(picks, el, NN)
        return 0

    lax.fori_loop(0, chunks, gather, 0)
    slope = jnp.zeros((group_rows, LANES), F32)
    for k in range(slabs):
        slope = slope + r_ref[k * group_rows : (k + 1) * group_rows, slab_cols:]
    for k in range(slabs):
        for b in range(band):
            span = slice(b * piece, (b + 1) * piece)
            part = r_ref[k * group_rows : (k + 1) * group_rows, span]
            part = part + slope[:, :1] * mass_ref[k : k + 1, span]
            if k == 0:
                first_ref[b, :group_rows, :] = part
            else:
                rest_ref[k - 1, b] = part
    r = lax.broadcasted_iota(I32, slope.shape, 0)
    l = lax.broadcasted_iota(I32, slope.shape, 1)
    slope_row = jnp.sum(jnp.where(r == l, slope, 0.0), axis=0, keepdims=True)
    tail = jnp.concatenate([slope_row] + [jnp.zeros((1, LANES), F32)] * (piece // LANES - 1), axis=1)
    for b in range(band):
        first_ref[b, group_rows:, :] = jnp.broadcast_to(tail, (8, piece))


def assemble(width, band, me, feats, mass):
    sources, features, count = feats.shape
    slabs, slab_cols = mass.shape
    group_rows = VARS // sources
    piece = slab_cols // band
    most = round_up(sources * (count + 8), CHUNK)
    codes = round_up(slabs * group_rows, LANES)
    return pl.pallas_call(
        functools.partial(assemble_kernel, width, band),
        out_shape=(
            jax.ShapeDtypeStruct((band, group_rows + 8, piece), F32),
            jax.ShapeDtypeStruct((slabs - 1, band, group_rows, piece), F32),
        ),
        in_specs=[SMEM, VMEM, VMEM],
        out_specs=(VMEM, VMEM),
        scratch_shapes=[
            pltpu.VMEM((sources, count, LANES), F32),
            pltpu.VMEM((most, slab_cols + LANES), F32),
            pltpu.VMEM((most, codes), F32),
            pltpu.VMEM((codes, slab_cols + LANES), F32),
        ],
        name="assemble",
    )(me, feats, mass)


def fetch(kinds, which, block, sem):
    for o, ref in enumerate(kinds):

        @pl.when(which == o)
        def _(ref=ref):
            pltpu.make_async_copy(ref, block, sem).start()


def landed(kinds, block, sem):
    pltpu.make_async_copy(kinds[0], block, sem).wait()


def forward_kernel(n, which_ref, full_ref, rhs_ref, *refs):
    diag, coup, (y_ref, send_ref, d_ref, c_ref, sems) = refs[:n], refs[n : 2 * n], refs[2 * n :]
    band, rows, piece = full_ref.shape
    fetch(diag, which_ref[0], d_ref, sems.at[0])
    fetch(coup, which_ref[1], c_ref, sems.at[1])
    landed(diag, d_ref, sems.at[0])
    y = jnp.zeros((rows, piece), F32)
    for b in range(band):
        span = slice(b * piece, (b + 1) * piece)
        y = y + mul3(halves(full_ref[b]), halves(d_ref[:, span]), NT)
    y_ref[...] = y
    yy = halves(y)
    landed(coup, c_ref, sems.at[1])
    for b in range(band):
        span = slice(b * piece, (b + 1) * piece)
        send_ref[b] = rhs_ref[b] - mul3(yy, halves(c_ref[span, :]), NT)


def turn_kernel(n, which_ref, full_ref, *refs):
    diag, (send_ref, d_ref, sems) = refs[:n], refs[n:]
    band, rows, piece = full_ref.shape
    fetch(diag, which_ref[0], d_ref, sems.at[0])
    landed(diag, d_ref, sems.at[0])
    y = jnp.zeros((rows, piece), F32)
    for b in range(band):
        span = slice(b * piece, (b + 1) * piece)
        y = y + mul3(halves(full_ref[b]), halves(d_ref[:, span]), NT)
    yy = halves(y)
    for b in range(band):
        span = slice(b * piece, (b + 1) * piece)
        send_ref[b] = mul3(yy, halves(d_ref[:, span]), NN)


def backward_kernel(n, which_ref, full_ref, y_ref, *refs):
    diag, coup, (send_ref, d_ref, c_ref, sems) = refs[:n], refs[n : 2 * n], refs[2 * n :]
    band, rows, piece = full_ref.shape
    fetch(coup, which_ref[1], c_ref, sems.at[1])
    fetch(diag, which_ref[0], d_ref, sems.at[0])
    landed(coup, c_ref, sems.at[1])
    left = y_ref[...]
    for b in range(band):
        span = slice(b * piece, (b + 1) * piece)
        left = left - mul3(halves(full_ref[b]), halves(c_ref[span, :]), NN)
    ll = halves(left)
    landed(diag, d_ref, sems.at[0])
    for b in range(band):
        span = slice(b * piece, (b + 1) * piece)
        send_ref[b] = mul3(ll, halves(d_ref[:, span]), NN)


def on_device(
    diag_inverse,
    coupling,
    elem_stiff,
    elem_mass,
    elem_dofs,
    elem_slab,
    elem_var,
    mode,
    mass_mode,
    eigenvalue,
):
    chain_len = lax.axis_size("chain")
    band_len = lax.axis_size("band")
    chain_pos = lax.axis_index("chain")
    band_pos = lax.axis_index("band")
    piece, slab_cols = diag_inverse.shape
    width, count = elem_dofs.shape
    group_rows = VARS // chain_len

    own_mass = lax.dynamic_slice_in_dim(mass_mode, band_pos * piece, piece, 0)
    both = jnp.stack([mode, own_mass])
    devices = chain_len * band_len
    tables = lax.all_to_all(
        jnp.broadcast_to(both[None], (devices,) + both.shape), ("chain", "band"), 0, 0, tiled=True
    )
    whole_mode = tables[:, 0].reshape(-1, LANES)
    whole_mass = tables[:, 1].reshape(chain_len, slab_cols)

    diag, coup = {0: diag_inverse}, {0: coupling}
    bit = chain_len // 2
    while bit:
        pairs = [(i, i ^ bit) for i in range(chain_len)]
        for held in (diag, coup):
            for o in list(held):
                held[o ^ bit] = lax.ppermute(held[o], "chain", pairs)
        bit //= 2
    diag = [diag[o] for o in range(chain_len)]
    coup = [coup[o] for o in range(chain_len)]

    feats = element_loads(
        chain_len,
        eigenvalue,
        whole_mode,
        elem_dofs,
        elem_slab.reshape(1, count),
        elem_var.reshape(1, count),
        elem_stiff,
        elem_mass,
    )
    gathered = lax.all_to_all(
        jnp.broadcast_to(feats[None], (chain_len,) + feats.shape), "chain", 0, 0, tiled=True
    )
    send, rest = assemble(width, band_len, chain_pos.reshape(1), gathered, whole_mass)

    def swap(blocks):
        return lax.all_to_all(blocks, "band", 0, 0, tiled=True)

    def spread(part):
        return swap(jnp.broadcast_to(part[None], (band_len,) + part.shape))

    panel = jax.ShapeDtypeStruct((band_len, group_rows, piece), F32)
    piece_of = jax.ShapeDtypeStruct((group_rows, piece), F32)
    d_scratch = pltpu.VMEM((piece, slab_cols), F32)
    c_scratch = pltpu.VMEM((slab_cols, piece), F32)
    sems = pltpu.SemaphoreType.DMA((2,))

    def which(d, c):
        return jnp.stack([chain_pos ^ d, chain_pos ^ c]).astype(I32)

    solved = []
    slope = None
    for k in range(chain_len):
        summed = jnp.sum(swap(send), axis=0)
        if k == 0:
            slope = summed[group_rows:]
            summed = summed[:group_rows]
        full = spread(summed)
        if k < chain_len - 1:
            y, send = pl.pallas_call(
                functools.partial(forward_kernel, chain_len),
                out_shape=(piece_of, panel),
                in_specs=[SMEM, VMEM, VMEM] + [HBM] * (2 * chain_len),
                out_specs=(VMEM, VMEM),
                scratch_shapes=[d_scratch, c_scratch, sems],
                name="forward",
            )(which(k, k + 1), full, rest[k], *diag, *coup)
            solved.append(y)
        else:
            send = pl.pallas_call(
                functools.partial(turn_kernel, chain_len),
                out_shape=panel,
                in_specs=[SMEM, VMEM] + [HBM] * chain_len,
                out_specs=VMEM,
                scratch_shapes=[d_scratch, sems],
                name="turn",
            )(which(k, k), full, *diag)
    results = [None] * chain_len
    for k in range(chain_len - 1, -1, -1):
        results[k] = jnp.sum(swap(send), axis=0)
        if k:
            send = pl.pallas_call(
                functools.partial(backward_kernel, chain_len),
                out_shape=panel,
                in_specs=[SMEM, VMEM, VMEM] + [HBM] * (2 * chain_len),
                out_specs=VMEM,
                scratch_shapes=[d_scratch, c_scratch, sems],
                name="backward",
            )(which(k - 1, k), spread(results[k]), solved[k - 1], *diag, *coup)

    outgoing = jnp.stack([jnp.concatenate([r, slope], axis=0) for r in results])
    arrived = lax.all_to_all(outgoing, "chain", 0, 0, tiled=True)
    eigvec_slope = arrived[:, :group_rows].reshape(VARS, piece)
    eigval_slope = arrived[:, group_rows, :group_rows].reshape(VARS)
    return (eigvec_slope, eigval_slope)


def solution(mesh):
    in_specs = (
        P(("chain", "band"), None),
        P("chain", "band"),
        P(None, None, ("chain", "band")),
        P(None, None, ("chain", "band")),
        P(None, ("chain", "band")),
        P(("chain", "band"), None),
        P(("chain", "band")),
        P(("chain", "band")),
        P("chain"),
        P(),
    )
    out_specs = (P(None, ("chain", "band")), P())
    return jax.shard_map(
        on_device, mesh=mesh, in_specs=in_specs, out_specs=out_specs, check_vma=False
    )
```

time: 1580 us -> 438 us (0.28)
  waiting for transfers between devices: 1050 us -> 142 us
  other arithmetic: 171 us -> 3.29 us
  local copies, waits for them, and re-layouts: 123 us -> 15.2 us
  matrix products: 94.3 us -> 0 us
  Pallas kernels: 0 us -> 79.8 us
  blocking collectives: 107 us -> 164 us
    psum x14 -> x0, waiting for transfers between devices: 1020 us -> none  [advance(): summed = lax.psum(partial_value, 'band')]
    all_to_all x0 -> x11, blocking collectives: none -> 164 us  [the longest x10 156 us: swap(): return lax.all_to_all(blocks, 'band', 0, 0, tiled=True)]
    scatter-add x1 -> x0, other arithmetic: 160 us -> none  [on_device(): assembled = jnp.zeros((VARS * slab_rows,), jnp.float32).at[got_index.resh...]
    dot_general x29 -> x0, matrix products: 94.3 us -> none  [the longest x7 26.9 us: forward_finish(): lax.dot_general(coupled, diag_inverse, contract, precision=highest, prefe...]
    pallas_call x0 -> x9, Pallas kernels: none -> 79.8 us  [the longest x1 28.9 us: assemble(): pl.pallas_call(functools.partial(assemble_kernel, width, band), out_shape...]
    all_gather x1 -> x0, blocking collectives: 70.1 us -> none  [on_device(): whole_mode = lax.all_gather(mode, ('chain', 'band'), axis=0, tiled=True)]
    gather x2 -> x0, local copies, waits for them, and re-layouts: 68 us -> none  [on_device(): mode_at = whole_mode[dof_index]]
    ppermute x14 -> x6, waiting for transfers between devices: 18.6 us -> 82.3 us  [on_device(): held[o ^ bit] = lax.ppermute(held[o], 'chain', pairs)]
  transfers between devices with their start and end apart: 30 -> 13, of which waited for: 29 -> 9; matrix products, arithmetic and copies ran while one was open for 2% -> 2% of each run, Pallas kernels for 0% -> 9%
where the time goes in v1:
time: 438 us; the launch traced here: 437 us
  blocking collectives  164 us (37%)
  waiting for transfers between devices  142 us (32%)
  Pallas kernels  79.8 us (18%)
  starting transfers between devices  31.1 us (7%)
  local copies, waits for them, and re-layouts  15.2 us (3%)
    all_to_all x10, blocking collectives, swap(): return lax.all_to_all(blocks, 'band', 0, 0, tiled=True)  156 us
    ppermute x6, waiting for transfers between devices, on_device(): held[o ^ bit] = lax.ppermute(held[o], 'chain', pairs)  82.3 us
    all_to_all x5, waiting for transfers between devices, swap(): return lax.all_to_all(blocks, 'band', 0, 0, tiled=True)  51.8 us
    pallas_call x1, Pallas kernels, assemble(): pl.pallas_call(functools.partial(assemble_kernel, width, band), out_shape...  28.9 us
    pallas_call x3, Pallas kernels, on_device(): pl.pallas_call(functools.partial(forward_kernel, chain_len), out_shape=(p...  21.1 us
    all_to_all x5, starting transfers between devices, swap(): return lax.all_to_all(blocks, 'band', 0, 0, tiled=True)  17.6 us
    pallas_call x3, Pallas kernels, on_device(): pl.pallas_call(functools.partial(backward_kernel, chain_len), out_shape=p...  14.4 us
    pallas_call x1, Pallas kernels, element_loads(): pl.pallas_call(functools.partial(loads_kernel, groups), out_shape=jax.Sha...  9.67 us
  transfers between devices with their start and end apart: 13, of which 9 were waited for; matrix products, arithmetic and copies ran while one was open for 2% of the time, Pallas kernels for 9%

profile of v1, /device:TPU:0, one launch (start us, length us, event | category | flops | bytes accessed | tf_op | source)
XLA Modules:
  0.0 437.2 jit_solution(755216847243769140)
XLA Ops:
  12.7 38.3 %collective-permute-done.4.refs_6_ = f32[2048,256]{1,0:T(8,128)} collective-permute-done((f32[2048,256]{1,0:T(8,128)}, f32[2048,256]{1,0:T(8,128)}, u32[]{:S(2)}, u32[]{:S(2)}) %collective-permute-start.4) | collective-permute-done | bytes 2097184 | tf_op jit(solution)/shard_map/ppermute | solution.py:306
  51.0 44.1 %collective-permute-done.1.refs_2_ = f32[256,2048]{1,0:T(8,128)S(1)} collective-permute-done((f32[256,2048]{1,0:T(8,128)}, f32[256,2048]{1,0:T(8,128)S(1)}, u32[]{:S(2)}, u32[]{:S(2)}) %collective-permute-start.1) | collective-permute-done | bytes 2097184 | tf_op jit(solution)/shard_map/ppermute | solution.py:306
  97.0 9.7 %loads.1 = f32[56,512]{1,0:T(8,128)} custom-call(f32[1]{0:T(128)S(6)} %copy.12.lam_ref, f32[64,128]{1,0:T(8,128)} %bitcast.25, s32[24,512]{1,0:T(8,128)} %dofs_ref.1, s32[1,512]{1,0:T(1,128)} %bitcast.27, s32[1,512]{1,0:T(1,128)} %bitcast.28, f32[24,24,512]{2,1,0:T(8,128)} %stiff_ref.1, f32[24,24,512]{2,1,0:T(8,128)} %mass_ref.1), custom_call_target="tpu_custom_call" | custom-call | tf_op jit(solution)/shard_map/loads/pallas_call | solution.py:95
  112.5 7.4 %all-to-all-done.1.feat_ref = f32[4,56,512]{2,1,0:T(8,128)S(1)} async-done(((f32[4,56,512]{2,1,0:T(8,128)}), f32[4,56,512]{2,1,0:T(8,128)S(1)}, u32[]{:S(2)}, u32[]{:S(2)}) %all-to-all-start.1) | async-done | bytes 458784 | tf_op jit(solution)/shard_map/all_to_all | solution.py:321
  120.7 28.9 %assemble.1 = (f32[8,56,256]{2,1,0:T(8,128)}, f32[3,8,48,256]{3,2,1,0:T(8,128)}) custom-call(s32[1]{0:T(128)} %bitcast.me_ref, f32[4,56,512]{2,1,0:T(8,128)} %copy-done.1, f32[4,2048]{1,0:T(4,128)} %reshape_squeeze.10.mass_ref), custom_call_target="tpu_custom_call" | custom-call | tf_op jit(solution)/shard_map/assemble/pallas_call | solution.py:191
  149.6 19.3 %all_to_all.90 = f32[8,56,256]{2,1,0:T(8,128)S(1)} all-to-all(f32[8,56,256]{2,1,0:T(8,128)} %get-tuple-element.10), channel_id=1, replica_groups=mesh['chain'=4,'band'=8] {'band'}, dimensions={0} | all-to-all | bytes 917504 | tf_op jit(solution)/shard_map/all_to_all | solution.py:327
  176.3 9.0 %all-to-all-done.3.full_ref = f32[8,48,256]{2,1,0:T(8,128)S(1)} async-done(((f32[8,48,256]{2,1,0:T(8,128)}), f32[8,48,256]{2,1,0:T(8,128)S(1)}, u32[]{:S(2)}, u32[]{:S(2)}) %all-to-all-start.3) | async-done | bytes 393248 | tf_op jit(solution)/shard_map/all_to_all | solution.py:327
  186.1 7.0 %forward.3 = (f32[48,256]{1,0:T(8,128)}, f32[8,48,256]{2,1,0:T(8,128)}) custom-call(s32[2]{0:T(128)} %pad_add_fusion.which_ref, f32[8,48,256]{2,1,0:T(8,128)} %copy-done.3, f32[8,48,256]{2,1,0:T(8,128)} %get-tuple-element.20.rhs_ref, f32[256,2048]{1,0:T(8,128)} %refs_0_.13, f32[256,2048]{1,0:T(8,128)} %collective-permute-done.refs_1_, f32[256,2048]{1,0:T(8,128)} %copy-done, ...), custom_call_target="tpu_custom_call" | custom-call | tf_op jit(solution)/shard_map/forward/pallas_call | solution.py:350
  193.1 15.9 %all_to_all.91 = f32[8,48,256]{2,1,0:T(8,128)S(1)} all-to-all(f32[8,48,256]{2,1,0:T(8,128)} %get-tuple-element.12), channel_id=1, replica_groups=mesh['chain'=4,'band'=8] {'band'}, dimensions={0} | all-to-all | bytes 786432 | tf_op jit(solution)/shard_map/all_to_all | solution.py:327
  213.9 10.7 %all-to-all-done.5.full_ref = f32[8,48,256]{2,1,0:T(8,128)S(1)} async-done(((f32[8,48,256]{2,1,0:T(8,128)}), f32[8,48,256]{2,1,0:T(8,128)S(1)}, u32[]{:S(2)}, u32[]{:S(2)}) %all-to-all-start.5) | async-done | bytes 393248 | tf_op jit(solution)/shard_map/all_to_all | solution.py:327
  225.4 7.0 %forward.4 = (f32[48,256]{1,0:T(8,128)}, f32[8,48,256]{2,1,0:T(8,128)}) custom-call(s32[2]{0:T(128)} %pad_add_fusion.1.which_ref, f32[8,48,256]{2,1,0:T(8,128)} %copy-done.5, f32[8,48,256]{2,1,0:T(8,128)} %get-tuple-element.19.rhs_ref, f32[256,2048]{1,0:T(8,128)} %refs_0_.13, f32[256,2048]{1,0:T(8,128)} %collective-permute-done.refs_1_, ...), custom_call_target="tpu_custom_call" | custom-call | tf_op jit(solution)/shard_map/forward/pallas_call | solution.py:350
  232.4 15.5 %all_to_all.92 = f32[8,48,256]{2,1,0:T(8,128)S(1)} all-to-all(f32[8,48,256]{2,1,0:T(8,128)} %get-tuple-element.13), channel_id=1, replica_groups=mesh['chain'=4,'band'=8] {'band'}, dimensions={0} | all-to-all | bytes 786432 | tf_op jit(solution)/shard_map/all_to_all | solution.py:327
  252.8 10.6 %all-to-all-done.7.full_ref = f32[8,48,256]{2,1,0:T(8,128)S(1)} async-done(((f32[8,48,256]{2,1,0:T(8,128)}), f32[8,48,256]{2,1,0:T(8,128)S(1)}, u32[]{:S(2)}, u32[]{:S(2)}) %all-to-all-start.7) | async-done | bytes 393248 | tf_op jit(solution)/shard_map/all_to_all | solution.py:327
  264.2 7.0 %forward.5 = (f32[48,256]{1,0:T(8,128)}, f32[8,48,256]{2,1,0:T(8,128)}) custom-call(s32[2]{0:T(128)} %pad_add_fusion.2.which_ref, f32[8,48,256]{2,1,0:T(8,128)} %copy-done.4, f32[8,48,256]{2,1,0:T(8,128)} %get-tuple-element.18.rhs_ref, f32[256,2048]{1,0:T(8,128)} %refs_0_.13, f32[256,2048]{1,0:T(8,128)} %collective-permute-done.refs_1_, ...), custom_call_target="tpu_custom_call" | custom-call | tf_op jit(solution)/shard_map/forward/pallas_call | solution.py:350
  271.3 15.5 %all_to_all.93 = f32[8,48,256]{2,1,0:T(8,128)S(1)} all-to-all(f32[8,48,256]{2,1,0:T(8,128)} %get-tuple-element.14), channel_id=1, replica_groups=mesh['chain'=4,'band'=8] {'band'}, dimensions={0} | all-to-all | bytes 786432 | tf_op jit(solution)/shard_map/all_to_all | solution.py:327
  291.8 10.4 %all-to-all-done.9.full_ref = f32[8,48,256]{2,1,0:T(8,128)S(1)} async-done(((f32[8,48,256]{2,1,0:T(8,128)}), f32[8,48,256]{2,1,0:T(8,128)S(1)}, u32[]{:S(2)}, u32[]{:S(2)}) %all-to-all-start.9) | async-done | bytes 393248 | tf_op jit(solution)/shard_map/all_to_all | solution.py:327
  308.7 15.5 %all_to_all.94 = f32[8,48,256]{2,1,0:T(8,128)S(1)} all-to-all(f32[8,48,256]{2,1,0:T(8,128)} %turn.1), channel_id=1, replica_groups=mesh['chain'=4,'band'=8] {'band'}, dimensions={0} | all-to-all | bytes 786432 | tf_op jit(solution)/shard_map/all_to_all | solution.py:327
  324.3 14.9 %all_to_all.95.full_ref = f32[8,48,256]{2,1,0:T(8,128)} all-to-all(f32[8,48,256]{2,1,0:T(8,128)S(1)} %broadcast_in_dim.24), channel_id=1, replica_groups=mesh['chain'=4,'band'=8] {'band'}, dimensions={0} | all-to-all | bytes 786432 | tf_op jit(solution)/shard_map/all_to_all | solution.py:327
  344.0 14.9 %all_to_all.96 = f32[8,48,256]{2,1,0:T(8,128)S(1)} all-to-all(f32[8,48,256]{2,1,0:T(8,128)} %backward.3), channel_id=1, replica_groups=mesh['chain'=4,'band'=8] {'band'}, dimensions={0} | all-to-all | bytes 786432 | tf_op jit(solution)/shard_map/all_to_all | solution.py:327
  359.1 14.8 %all_to_all.97.full_ref = f32[8,48,256]{2,1,0:T(8,128)} all-to-all(f32[8,48,256]{2,1,0:T(8,128)S(1)} %broadcast_in_dim.25), channel_id=1, replica_groups=mesh['chain'=4,'band'=8] {'band'}, dimensions={0} | all-to-all | bytes 786432 | tf_op jit(solution)/shard_map/all_to_all | solution.py:327
  378.7 14.9 %all_to_all.98 = f32[8,48,256]{2,1,0:T(8,128)S(1)} all-to-all(f32[8,48,256]{2,1,0:T(8,128)} %backward.4), channel_id=1, replica_groups=mesh['chain'=4,'band'=8] {'band'}, dimensions={0} | all-to-all | bytes 786432 | tf_op jit(solution)/shard_map/all_to_all | solution.py:327
  393.6 14.8 %all_to_all.99.full_ref = f32[8,48,256]{2,1,0:T(8,128)} all-to-all(f32[8,48,256]{2,1,0:T(8,128)S(1)} %broadcast_in_dim.26), channel_id=1, replica_groups=mesh['chain'=4,'band'=8] {'band'}, dimensions={0} | all-to-all | bytes 786432 | tf_op jit(solution)/shard_map/all_to_all | solution.py:327
  416.7 11.0 %all-to-all-done.16 = f32[8,48,256]{2,1,0:T(8,128)S(1)} async-done(((f32[8,48,256]{2,1,0:T(8,128)}), f32[8,48,256]{2,1,0:T(8,128)S(1)}, u32[]{:S(2)}, u32[]{:S(2)}) %all-to-all-start.16) | async-done | bytes 393248 | tf_op jit(solution)/shard_map/all_to_all | solution.py:327
  427.8 8.0 %all_to_all.100 = f32[4,56,256]{2,1,0:T(8,128)S(1)} all-to-all(f32[4,56,256]{2,1,0:T(8,128)S(1)} %pad_maximum_fusion), channel_id=1, replica_groups=mesh['chain'=4,'band'=8] {'chain'}, dimensions={0} | all-to-all | bytes 458752 | tf_op jit(solution)/shard_map/all_to_all | solution.py:382
  (67 shorter events, 70.2 us)
Async XLA Ops:
  0.6 50.4 %collective-permute-start.4 = (f32[2048,256]{1,0:T(8,128)}, f32[2048,256]{1,0:T(8,128)}, u32[]{:S(2)}, u32[]{:S(2)}) collective-permute-start(f32[2048,256]{1,0:T(8,128)} %refs_4_.11), channel_id=1, source_target_pairs={{0,16},{8,24},{16,0},{24,8},{1,17},{9,25},{17,1},{25,9},{2,18},{10... | collective-permute-start | bytes 6291464 | tf_op jit(solution)/shard_map/ppermute | solution.py:306
  3.7 91.4 %collective-permute-start.1 = (f32[256,2048]{1,0:T(8,128)}, f32[256,2048]{1,0:T(8,128)S(1)}, u32[]{:S(2)}, u32[]{:S(2)}) collective-permute-start(f32[256,2048]{1,0:T(8,128)} %refs_0_.13), channel_id=1, source_target_pairs={{0,16},{8,24},{16,0},{24,8},{1,17},{9,25},{17,1},{25,9},{2,18},{10... | collective-permute-start | bytes 6291464 | tf_op jit(solution)/shard_map/ppermute | solution.py:306
  5.8 90.5 %all-to-all-start = ((f32[32,2,256]{2,1,0:T(2,128)}), f32[32,2,256]{2,1,0:T(2,128)S(1)}, u32[]{:S(2)}, u32[]{:S(2)}) async-start(f32[32,2,256]{2,1,0:T(2,128)} %broadcast_in_dim.18), calls=%async_computation | async-start | bytes 131072 | tf_op jit(solution)/shard_map/all_to_all | solution.py:294
  12.1 173.2 %collective-permute-start.3 = (f32[2048,256]{1,0:T(8,128)}, f32[2048,256]{1,0:T(8,128)}, u32[]{:S(2)}, u32[]{:S(2)}) collective-permute-start(f32[2048,256]{1,0:T(8,128)} %refs_4_.11), channel_id=1, source_target_pairs={{0,8},{8,0},{16,24},{24,16},{1,9},{9,1},{17,25},{25,17},{2,10},{10... | collective-permute-start | bytes 6291464 | tf_op jit(solution)/shard_map/ppermute | solution.py:306
  12.5 172.9 %collective-permute-start = (f32[256,2048]{1,0:T(8,128)}, f32[256,2048]{1,0:T(8,128)}, u32[]{:S(2)}, u32[]{:S(2)}) collective-permute-start(f32[256,2048]{1,0:T(8,128)} %refs_0_.13), channel_id=1, source_target_pairs={{0,8},{8,0},{16,24},{24,16},{1,9},{9,1},{17,25},{25,17},{2,10},{10... | collective-permute-start | bytes 6291464 | tf_op jit(solution)/shard_map/ppermute | solution.py:306
  51.0 134.4 %collective-permute-start.5 = (f32[2048,256]{1,0:T(8,128)}, f32[2048,256]{1,0:T(8,128)}, u32[]{:S(2)}, u32[]{:S(2)}) collective-permute-start(f32[2048,256]{1,0:T(8,128)} %collective-permute-done.4.refs_6_), channel_id=1, source_target_pairs={{0,8},{8,0},{16,24},{24,16},{1,9},{9,1},{17,25},{25,17},{2,10},{10... | collective-permute-start | bytes 6291464 | tf_op jit(solution)/shard_map/ppermute | solution.py:306
  95.1 16.8 %copy-start = (f32[256,2048]{1,0:T(8,128)}, f32[256,2048]{1,0:T(8,128)S(1)}, u32[]{:S(2)}) copy-start(f32[256,2048]{1,0:T(8,128)S(1)} %collective-permute-done.1.refs_2_) | copy-start | bytes 6291460
  95.1 90.3 %collective-permute-start.2 = (f32[256,2048]{1,0:T(8,128)S(1)}, f32[256,2048]{1,0:T(8,128)}, u32[]{:S(2)}, u32[]{:S(2)}) collective-permute-start(f32[256,2048]{1,0:T(8,128)S(1)} %collective-permute-done.1.refs_2_), channel_id=1, source_target_pairs={{0,8},{8,0},{16,24},{24,16},{1,9},{9,1},{17,25},{25,17},{2,10},{10... | collective-permute-start | bytes 6291464 | tf_op jit(solution)/shard_map/ppermute | solution.py:306
  108.4 11.6 %all-to-all-start.1 = ((f32[4,56,512]{2,1,0:T(8,128)}), f32[4,56,512]{2,1,0:T(8,128)S(1)}, u32[]{:S(2)}, u32[]{:S(2)}) async-start(f32[4,56,512]{2,1,0:T(8,128)} %broadcast_in_dim.19), calls=%async_computation.1 | async-start | bytes 917504 | tf_op jit(solution)/shard_map/all_to_all | solution.py:321
  119.9 0.8 copy-start.1
  169.8 15.6 %all-to-all-start.3 = ((f32[8,48,256]{2,1,0:T(8,128)}), f32[8,48,256]{2,1,0:T(8,128)S(1)}, u32[]{:S(2)}, u32[]{:S(2)}) async-start(f32[8,48,256]{2,1,0:T(8,128)} %broadcast_in_dim.20), calls=%async_computation.3 | async-start | bytes 786432 | tf_op jit(solution)/shard_map/all_to_all | solution.py:327
  185.4 0.8 copy-start.3
  209.8 14.8 %all-to-all-start.5 = ((f32[8,48,256]{2,1,0:T(8,128)}), f32[8,48,256]{2,1,0:T(8,128)S(1)}, u32[]{:S(2)}, u32[]{:S(2)}) async-start(f32[8,48,256]{2,1,0:T(8,128)} %broadcast_in_dim.21), calls=%async_computation.5 | async-start | bytes 786432 | tf_op jit(solution)/shard_map/all_to_all | solution.py:327
  224.6 0.8 copy-start.5
  248.8 14.6 %all-to-all-start.7 = ((f32[8,48,256]{2,1,0:T(8,128)}), f32[8,48,256]{2,1,0:T(8,128)S(1)}, u32[]{:S(2)}, u32[]{:S(2)}) async-start(f32[8,48,256]{2,1,0:T(8,128)} %broadcast_in_dim.22), calls=%async_computation.7 | async-start | bytes 786432 | tf_op jit(solution)/shard_map/all_to_all | solution.py:327
  263.4 0.8 copy-start.4
  287.6 14.6 %all-to-all-start.9 = ((f32[8,48,256]{2,1,0:T(8,128)}), f32[8,48,256]{2,1,0:T(8,128)S(1)}, u32[]{:S(2)}, u32[]{:S(2)}) async-start(f32[8,48,256]{2,1,0:T(8,128)} %broadcast_in_dim.23), calls=%async_computation.9 | async-start | bytes 786432 | tf_op jit(solution)/shard_map/all_to_all | solution.py:327
  302.3 0.8 copy-start.2
  413.2 14.5 %all-to-all-start.16 = ((f32[8,48,256]{2,1,0:T(8,128)}), f32[8,48,256]{2,1,0:T(8,128)S(1)}, u32[]{:S(2)}, u32[]{:S(2)}) async-start(f32[8,48,256]{2,1,0:T(8,128)} %backward.5), calls=%async_computation.16 | async-start | bytes 786432 | tf_op jit(solution)/shard_map/all_to_all | solution.py:327
